TPU v7x, 512 devices: a whole 4x4x16 slice. The times are simulated.
512 devices in a mesh: ship: 64 (over x, z_hi, y), trans: 4 (over z_lo), vert: 2 (over core).
Axes of the slice: x: 4, y: 4, z: 16 (z_hi: 4, z_lo: 4; z = z_hi * 4 + z_lo), core: 2. Of those that a mesh axis runs over, the one named last changes fastest.
Arguments:
- potential: float32 [64, 1024, 512], P('vert', 'ship', 'trans'), may hold values from -6 to 6
- source: float32 [64, 1024, 512], P('vert', 'ship', 'trans'), may hold values from -6 to 6
- stencil: bfloat16 [27, 64, 1024, 512], P(None, 'vert', 'ship', 'trans'), may hold values from -4.6 to 0.1, as said below
- surface_potential: float32 [1024, 512], P(('ship', 'vert'), 'trans'), may hold values from -6 to 6
- elevation: float32 [1024, 512], P(('ship', 'vert'), 'trans'), may hold values from -0.2 to 0.2
- hull_mask: int32 [1024, 512], P(('ship', 'vert'), 'trans'), may hold values 0 or 1
- column_inverse: float32 [2, 64, 64], replicated, may hold values from -0.3 to 0.03
Outputs:
- updated: float32 [64, 1024, 512], P('vert', 'ship', 'trans')
- residual: float32 [64, 1024, 512], P('vert', 'ship', 'trans')
Inputs may be any that keep to these rules, and one draw needn't show every extreme that they name: `stencil`: entry 13 of the first dimension (the centre) lies between -4.6 and -3.0 at every cell, the other 26 entries between 0 and 0.1. `hull_mask`: 1 marks a column under a hull panel.
All inputs are finite; a program needn't handle non-finite values. No bound on the sum of `hull_mask` on one device may be relied on, other than what follows from the above.
Results may differ from a plain program's by a relative error of at most 0.0003.
Values may be sent and summed in bfloat16 or wider, within the bound.
A program may use at most 64 MiB of HBM per device.

v0:
```python
import jax
import jax.numpy as jnp
from jax import lax
from jax.sharding import PartitionSpec as P

SWEEPS = 4


def partner(block, axis, distance):
    count = lax.axis_size(axis)
    route = []
    for low in range(count):
        high = low | 1 << distance
        if high != low and high < count:
            route += [(low, high), (high, low)]
    return lax.ppermute(block, axis, route)


def extended_2(cells, sides, width):
    for axis, dim in sides:
        count = lax.axis_size(axis)
        ends = count - 1
        head = lax.slice_in_dim(cells, 0, width, axis=dim)
        tail = lax.slice_in_dim(cells, cells.shape[dim] - width, cells.shape[dim], axis=dim)
        cells = jnp.concatenate(
            [
                lax.ppermute(tail, axis, [(i, (i + 1) % count) for i in range(ends)]),
                cells,
                lax.ppermute(head, axis, [((i + 1) % count, i) for i in range(ends)]),
            ],
            axis=dim,
        )
    return cells


def stencil_apply(padded, stencil):
    levels, row_count, col_count = (stencil.shape[1], stencil.shape[2], stencil.shape[3])
    summed = jnp.zeros((levels, row_count, col_count), jnp.float32)
    for offset_z in range(3):
        for offset_x in range(3):
            for offset_y in range(3):
                offset_index = 9 * offset_z + 3 * offset_x + offset_y
                window = padded[
                    offset_z : offset_z + levels,
                    offset_x : offset_x + row_count,
                    offset_y : offset_y + col_count,
                ]
                summed = summed + stencil[offset_index].astype(jnp.float32) * window
    return summed


def join_halves(vert_index, own_half, other_half):
    return jnp.where(
        vert_index == 0,
        jnp.concatenate([own_half, other_half], axis=0),
        jnp.concatenate([other_half, own_half], axis=0),
    )


def project(column_inverse, hull_weight, weight, vector_field):
    flattened = vector_field.reshape(vector_field.shape[0], -1)
    free_part = jnp.dot(
        column_inverse[0],
        flattened,
        precision=lax.Precision.HIGHEST,
        preferred_element_type=jnp.float32,
    ).reshape(vector_field.shape)
    hull_part = jnp.dot(
        column_inverse[1],
        flattened,
        precision=lax.Precision.HIGHEST,
        preferred_element_type=jnp.float32,
    ).reshape(vector_field.shape)
    return weight * jnp.where(hull_weight > 0.5, hull_part, free_part)


def to_slabs(increment):
    return lax.all_to_all(increment, "vert", split_axis=0, concat_axis=1, tiled=True)


def per_device(potential, source, stencil, surface_potential, elevation, hull_mask, column_inverse):
    vert_index = lax.axis_index("vert")
    half_hull = hull_mask.astype(jnp.float32)
    boundary_face = jnp.where(vert_index == 0, potential[-1], potential[0])
    partner_face, partner_surface, partner_hull = partner(
        (boundary_face, surface_potential, half_hull), "vert", 0
    )
    full_surface = join_halves(vert_index, surface_potential, partner_surface)
    full_hull = join_halves(vert_index, half_hull, partner_hull)

    def slab_extend(field_values, partner_layer, top_value):
        below_layer = jnp.where(vert_index == 0, field_values[0], partner_layer)
        surface_layer = full_hull * field_values[-1] + (1.0 - full_hull) * top_value
        above_layer = jnp.where(vert_index == 0, partner_layer, surface_layer)
        return jnp.concatenate([below_layer[None], field_values, above_layer[None]], axis=0)

    extended = slab_extend(potential, partner_face, full_surface)
    padded = extended_2(extended, (("ship", 1), ("trans", 2)), 1)
    residual = source - stencil_apply(padded, stencil)
    weight = 0.5 * (1.0 + elevation) * (1.0 + elevation)
    columns_residual = lax.all_to_all(residual, "vert", split_axis=1, concat_axis=0, tiled=True)
    increment = project(column_inverse, half_hull, weight, columns_residual)
    correction = to_slabs(increment)
    zero_top = jnp.zeros_like(full_surface)
    for sweep_index in range(SWEEPS - 1):
        correction_face = jnp.where(vert_index == 0, correction[-1], correction[0])
        partner_layer = partner(correction_face, "vert", 0)
        correction_ext = slab_extend(correction, partner_layer, zero_top)
        correction_pad = extended_2(correction_ext, (("ship", 1), ("trans", 2)), 1)
        defect = residual - stencil_apply(correction_pad, stencil)
        columns_defect = lax.all_to_all(defect, "vert", split_axis=1, concat_axis=0, tiled=True)
        correction = correction + to_slabs(
            project(column_inverse, half_hull, weight, columns_defect)
        )
    return (potential + correction, residual)


def solution(mesh):
    return jax.shard_map(
        per_device,
        mesh=mesh,
        in_specs=(
            P("vert", "ship", "trans"),
            P("vert", "ship", "trans"),
            P(None, "vert", "ship", "trans"),
            P(("ship", "vert"), "trans"),
            P(("ship", "vert"), "trans"),
            P(("ship", "vert"), "trans"),
            P(),
        ),
        out_specs=(P("vert", "ship", "trans"), P("vert", "ship", "trans")),
        check_vma=False,
    )
```

profile of v0, /device:TPU:7, one launch (start us, length us, event | category | flops | bytes accessed | tf_op | source)
XLA Modules:
  0.0 192.4 jit_solution(17414575642090886000)
XLA Ops:
  1.5 2.7 %collective-permute-start = (f32[16,128]{1,0:T(8,128)S(1)}, f32[16,128]{1,0:T(8,128)S(1)}, u32[]{:S(2)}, u32[]{:S(2)}) collective-permute-start(f32[16,128]{1,0:T(8,128)S(1)} %bitcast_select_fusion.4), channel_id=1, source_target_pairs={{0,1},{1,0},{2,3},{3,2},{4,5},{5,4},{6,7},{7,6},{8,9},{9,8},{10,11... | collective-permute-start | bytes 24584 | tf_op jit(solution)/shard_map/ppermute | solution.py:16
  12.1 3.2 %collective-permute-start.3 = (f32[34,1,128]{2,1,0:T(1,128)S(1)}, f32[34,1,128]{2,1,0:T(1,128)S(1)}, u32[]{:S(2)}, u32[]{:S(2)}) collective-permute-start(f32[34,1,128]{2,1,0:T(1,128)S(1)} %get-tuple-element.53), channel_id=1, source_target_pairs={{0,8},{8,16},{16,24},{24,32},{32,40},{40,48},{48,56},{56,64},{64,7... | collective-permute-start | bytes 52232 | tf_op jit(solution)/shard_map/ppermute | solution.py:27
  15.3 13.9 %collective-permute-start.4 = (f32[34,1,128]{2,1,0:T(1,128)S(1)}, f32[34,1,128]{2,1,0:T(1,128)S(1)}, u32[]{:S(2)}, u32[]{:S(2)}) collective-permute-start(f32[34,1,128]{2,1,0:T(1,128)S(1)} %get-tuple-element.54), channel_id=1, source_target_pairs={{8,0},{16,8},{24,16},{32,24},{40,32},{48,40},{56,48},{64,56},{72,6... | collective-permute-start | bytes 52232 | tf_op jit(solution)/shard_map/ppermute | solution.py:29
  31.2 2.7 %collective-permute-start.5 = (f32[34,18,1]{2,1,0:T(8,128)S(1)}, f32[34,18,1]{2,1,0:T(8,128)S(1)}, u32[]{:S(2)}, u32[]{:S(2)}) collective-permute-start(f32[34,18,1]{2,1,0:T(8,128)S(1)} %get-tuple-element.33), channel_id=1, source_target_pairs={{0,2},{2,4},{4,6},{1,3},{3,5},{5,7},{8,10},{10,12},{12,14},{9,11},... | collective-permute-start | bytes 7352 | tf_op jit(solution)/shard_map/ppermute | solution.py:27
  36.3 5.3 %collective-permute-done.5 = f32[34,18,1]{2,1,0:T(8,128)S(1)} collective-permute-done((f32[34,18,1]{2,1,0:T(8,128)S(1)}, f32[34,18,1]{2,1,0:T(8,128)S(1)}, u32[]{:S(2)}, u32[]{:S(2)}) %collective-permute-start.5) | collective-permute-done | bytes 2480 | tf_op jit(solution)/shard_map/ppermute | solution.py:27
  41.7 3.9 %collective-permute-done.6 = f32[34,18,1]{2,1,0:T(8,128)S(1)} collective-permute-done((f32[34,18,1]{2,1,0:T(8,128)S(1)}, f32[34,18,1]{2,1,0:T(8,128)S(1)}, u32[]{:S(2)}, u32[]{:S(2)}) %collective-permute-start.6) | collective-permute-done | bytes 2480 | tf_op jit(solution)/shard_map/ppermute | solution.py:29
  47.2 5.9 %all_to_all.132 = f32[32,16,128]{2,0,1:T(8,128)S(1)} all-to-all(f32[32,16,128]{2,0,1:T(8,128)S(1)} %copy_subtract_fusion), channel_id=1, replica_groups=mesh['ship'=64,'trans'=4,'vert'=2] {'vert'}, dimensions={1} | all-to-all | bytes 524288 | tf_op jit(solution)/shard_map/all_to_all | solution.py:101
  54.3 3.9 %all_to_all.133 = f32[64,8,128]{2,1,0:T(8,128)S(1)} all-to-all(f32[64,8,128]{2,1,0:T(8,128)S(1)} %fusion.99), channel_id=1, replica_groups=mesh['ship'=64,'trans'=4,'vert'=2] {'vert'}, dimensions={0} | all-to-all | bytes 524288 | tf_op jit(solution)/shard_map/all_to_all | solution.py:78
  63.3 10.6 %collective-permute-start.9 = (f32[34,1,128]{2,1,0:T(1,128)S(1)}, f32[34,1,128]{2,1,0:T(1,128)S(1)}, u32[]{:S(2)}, u32[]{:S(2)}) collective-permute-start(f32[34,1,128]{2,1,0:T(1,128)S(1)} %get-tuple-element.50), channel_id=1, source_target_pairs={{8,0},{16,8},{24,16},{32,24},{40,32},{48,40},{56,48},{64,56},{72,6... | collective-permute-start | bytes 52232 | tf_op jit(solution)/shard_map/ppermute | solution.py:29
  75.0 2.9 %collective-permute-start.10 = (f32[34,18,1]{2,1,0:T(8,128)S(1)}, f32[34,18,1]{2,1,0:T(8,128)S(1)}, u32[]{:S(2)}, u32[]{:S(2)}) collective-permute-start(f32[34,18,1]{2,1,0:T(8,128)S(1)} %get-tuple-element.31), channel_id=1, source_target_pairs={{0,2},{2,4},{4,6},{1,3},{3,5},{5,7},{8,10},{10,12},{12,14},{9,11},... | collective-permute-start | bytes 7352 | tf_op jit(solution)/shard_map/ppermute | solution.py:27
  79.2 6.4 %collective-permute-done.10 = f32[34,18,1]{2,1,0:T(8,128)S(1)} collective-permute-done((f32[34,18,1]{2,1,0:T(8,128)S(1)}, f32[34,18,1]{2,1,0:T(8,128)S(1)}, u32[]{:S(2)}, u32[]{:S(2)}) %collective-permute-start.10) | collective-permute-done | bytes 2480 | tf_op jit(solution)/shard_map/ppermute | solution.py:27
  85.6 3.9 %collective-permute-done.11 = f32[34,18,1]{2,1,0:T(8,128)S(1)} collective-permute-done((f32[34,18,1]{2,1,0:T(8,128)S(1)}, f32[34,18,1]{2,1,0:T(8,128)S(1)}, u32[]{:S(2)}, u32[]{:S(2)}) %collective-permute-start.11) | collective-permute-done | bytes 2480 | tf_op jit(solution)/shard_map/ppermute | solution.py:29
  91.2 5.9 %all_to_all.134 = f32[32,16,128]{2,0,1:T(8,128)S(1)} all-to-all(f32[32,16,128]{2,0,1:T(8,128)S(1)} %copy.26), channel_id=1, replica_groups=mesh['ship'=64,'trans'=4,'vert'=2] {'vert'}, dimensions={1} | all-to-all | bytes 524288 | tf_op jit(solution)/shard_map/all_to_all | solution.py:111
  98.2 3.9 %all_to_all.135 = f32[64,8,128]{2,1,0:T(8,128)S(1)} all-to-all(f32[64,8,128]{2,1,0:T(8,128)S(1)} %fusion.96), channel_id=1, replica_groups=mesh['ship'=64,'trans'=4,'vert'=2] {'vert'}, dimensions={0} | all-to-all | bytes 524288 | tf_op jit(solution)/shard_map/all_to_all | solution.py:78
  107.3 10.6 %collective-permute-start.14 = (f32[34,1,128]{2,1,0:T(1,128)S(1)}, f32[34,1,128]{2,1,0:T(1,128)S(1)}, u32[]{:S(2)}, u32[]{:S(2)}) collective-permute-start(f32[34,1,128]{2,1,0:T(1,128)S(1)} %get-tuple-element.46), channel_id=1, source_target_pairs={{8,0},{16,8},{24,16},{32,24},{40,32},{48,40},{56,48},{64,56},{72,6... | collective-permute-start | bytes 52232 | tf_op jit(solution)/shard_map/ppermute | solution.py:29
  119.0 2.7 %collective-permute-start.15 = (f32[34,18,1]{2,1,0:T(8,128)S(1)}, f32[34,18,1]{2,1,0:T(8,128)S(1)}, u32[]{:S(2)}, u32[]{:S(2)}) collective-permute-start(f32[34,18,1]{2,1,0:T(8,128)S(1)} %get-tuple-element.29), channel_id=1, source_target_pairs={{0,2},{2,4},{4,6},{1,3},{3,5},{5,7},{8,10},{10,12},{12,14},{9,11},... | collective-permute-start | bytes 7352 | tf_op jit(solution)/shard_map/ppermute | solution.py:27
  123.1 6.4 %collective-permute-done.15 = f32[34,18,1]{2,1,0:T(8,128)S(1)} collective-permute-done((f32[34,18,1]{2,1,0:T(8,128)S(1)}, f32[34,18,1]{2,1,0:T(8,128)S(1)}, u32[]{:S(2)}, u32[]{:S(2)}) %collective-permute-start.15) | collective-permute-done | bytes 2480 | tf_op jit(solution)/shard_map/ppermute | solution.py:27
  129.5 3.9 %collective-permute-done.16 = f32[34,18,1]{2,1,0:T(8,128)S(1)} collective-permute-done((f32[34,18,1]{2,1,0:T(8,128)S(1)}, f32[34,18,1]{2,1,0:T(8,128)S(1)}, u32[]{:S(2)}, u32[]{:S(2)}) %collective-permute-start.16) | collective-permute-done | bytes 2480 | tf_op jit(solution)/shard_map/ppermute | solution.py:29
  134.9 5.9 %all_to_all.136 = f32[32,16,128]{2,0,1:T(8,128)S(1)} all-to-all(f32[32,16,128]{2,0,1:T(8,128)S(1)} %copy.30), channel_id=1, replica_groups=mesh['ship'=64,'trans'=4,'vert'=2] {'vert'}, dimensions={1} | all-to-all | bytes 524288 | tf_op jit(solution)/shard_map/all_to_all | solution.py:111
  142.0 3.9 %all_to_all.137 = f32[64,8,128]{2,1,0:T(8,128)S(1)} all-to-all(f32[64,8,128]{2,1,0:T(8,128)S(1)} %fusion.93), channel_id=1, replica_groups=mesh['ship'=64,'trans'=4,'vert'=2] {'vert'}, dimensions={0} | all-to-all | bytes 524288 | tf_op jit(solution)/shard_map/all_to_all | solution.py:78
  151.1 10.6 %collective-permute-start.19 = (f32[34,1,128]{2,1,0:T(1,128)S(1)}, f32[34,1,128]{2,1,0:T(1,128)S(1)}, u32[]{:S(2)}, u32[]{:S(2)}) collective-permute-start(f32[34,1,128]{2,1,0:T(1,128)S(1)} %get-tuple-element.42), channel_id=1, source_target_pairs={{8,0},{16,8},{24,16},{32,24},{40,32},{48,40},{56,48},{64,56},{72,6... | collective-permute-start | bytes 52232 | tf_op jit(solution)/shard_map/ppermute | solution.py:29
  166.4 10.2 %collective-permute-done.21 = f32[34,18,1]{2,1,0:T(8,128)S(1)} collective-permute-done((f32[34,18,1]{2,1,0:T(8,128)S(1)}, f32[34,18,1]{2,1,0:T(8,128)S(1)}, u32[]{:S(2)}, u32[]{:S(2)}) %collective-permute-start.21) | collective-permute-done | bytes 2480 | tf_op jit(solution)/shard_map/ppermute | solution.py:29
  180.7 5.9 %all_to_all.138 = f32[32,16,128]{2,0,1:T(8,128)S(1)} all-to-all(f32[32,16,128]{2,0,1:T(8,128)S(1)} %fusion.103), channel_id=1, replica_groups=mesh['ship'=64,'trans'=4,'vert'=2] {'vert'}, dimensions={1} | all-to-all | bytes 524288 | tf_op jit(solution)/shard_map/all_to_all | solution.py:111
  187.7 3.9 %all_to_all.139 = f32[64,8,128]{2,1,0:T(8,128)S(1)} all-to-all(f32[64,8,128]{2,1,0:T(8,128)S(1)} %fusion.90), channel_id=1, replica_groups=mesh['ship'=64,'trans'=4,'vert'=2] {'vert'}, dimensions={0} | all-to-all | bytes 524288 | tf_op jit(solution)/shard_map/all_to_all | solution.py:78
  (115 shorter events, 52.1 us)
Async XLA Ops:
  0.6 45.4 %copy-start = (bf16[27,32,16,128]{3,2,1,0:T(8,128)(2,1)S(1)}, bf16[27,32,16,128]{3,2,1,0:T(8,128)(2,1)}, u32[]{:S(2)}) copy-start(bf16[27,32,16,128]{3,2,1,0:T(8,128)(2,1)} %param.9) | copy-start | bytes 10616836
  0.6 44.9 %copy-start.1 = (f32[32,16,128]{2,1,0:T(8,128)S(1)}, f32[32,16,128]{2,1,0:T(8,128)}, u32[]{:S(2)}) copy-start(f32[32,16,128]{2,1,0:T(8,128)} %param.7) | copy-start | bytes 786436
  1.5 8.8 %collective-permute-start = (f32[16,128]{1,0:T(8,128)S(1)}, f32[16,128]{1,0:T(8,128)S(1)}, u32[]{:S(2)}, u32[]{:S(2)}) collective-permute-start(f32[16,128]{1,0:T(8,128)S(1)} %bitcast_select_fusion.4), channel_id=1, source_target_pairs={{0,1},{1,0},{2,3},{3,2},{4,5},{5,4},{6,7},{7,6},{8,9},{9,8},{10,11... | collective-permute-start | bytes 24584 | tf_op jit(solution)/shard_map/ppermute | solution.py:16
  4.9 5.0 %collective-permute-start.1 = (f32[8,128]{1,0:T(8,128)S(1)}, f32[8,128]{1,0:T(8,128)S(1)}, u32[]{:S(2)}, u32[]{:S(2)}) collective-permute-start(f32[8,128]{1,0:T(8,128)S(1)} %convert_element_type.246), channel_id=1, source_target_pairs={{0,1},{1,0},{2,3},{3,2},{4,5},{5,4},{6,7},{7,6},{8,9},{9,8},{10,11... | collective-permute-start | bytes 12296 | tf_op jit(solution)/shard_map/ppermute | solution.py:16
  6.9 3.4 %collective-permute-start.2 = (f32[8,128]{1,0:T(8,128)}, f32[8,128]{1,0:T(8,128)S(1)}, u32[]{:S(2)}, u32[]{:S(2)}) collective-permute-start(f32[8,128]{1,0:T(8,128)} %param.10), channel_id=1, source_target_pairs={{0,1},{1,0},{2,3},{3,2},{4,5},{5,4},{6,7},{7,6},{8,9},{9,8},{10,11... | collective-permute-start | bytes 12296 | tf_op jit(solution)/shard_map/ppermute | solution.py:16
  12.1 17.8 %collective-permute-start.3 = (f32[34,1,128]{2,1,0:T(1,128)S(1)}, f32[34,1,128]{2,1,0:T(1,128)S(1)}, u32[]{:S(2)}, u32[]{:S(2)}) collective-permute-start(f32[34,1,128]{2,1,0:T(1,128)S(1)} %get-tuple-element.53), channel_id=1, source_target_pairs={{0,8},{8,16},{16,24},{24,32},{32,40},{40,48},{48,56},{56,64},{64,7... | collective-permute-start | bytes 52232 | tf_op jit(solution)/shard_map/ppermute | solution.py:27
  15.3 14.8 %collective-permute-start.4 = (f32[34,1,128]{2,1,0:T(1,128)S(1)}, f32[34,1,128]{2,1,0:T(1,128)S(1)}, u32[]{:S(2)}, u32[]{:S(2)}) collective-permute-start(f32[34,1,128]{2,1,0:T(1,128)S(1)} %get-tuple-element.54), channel_id=1, source_target_pairs={{8,0},{16,8},{24,16},{32,24},{40,32},{48,40},{56,48},{64,56},{72,6... | collective-permute-start | bytes 52232 | tf_op jit(solution)/shard_map/ppermute | solution.py:29
  31.2 10.4 %collective-permute-start.5 = (f32[34,18,1]{2,1,0:T(8,128)S(1)}, f32[34,18,1]{2,1,0:T(8,128)S(1)}, u32[]{:S(2)}, u32[]{:S(2)}) collective-permute-start(f32[34,18,1]{2,1,0:T(8,128)S(1)} %get-tuple-element.33), channel_id=1, source_target_pairs={{0,2},{2,4},{4,6},{1,3},{3,5},{5,7},{8,10},{10,12},{12,14},{9,11},... | collective-permute-start | bytes 7352 | tf_op jit(solution)/shard_map/ppermute | solution.py:27
  33.9 11.6 %collective-permute-start.6 = (f32[34,18,1]{2,1,0:T(8,128)S(1)}, f32[34,18,1]{2,1,0:T(8,128)S(1)}, u32[]{:S(2)}, u32[]{:S(2)}) collective-permute-start(f32[34,18,1]{2,1,0:T(8,128)S(1)} %get-tuple-element.34), channel_id=1, source_target_pairs={{2,0},{4,2},{6,4},{3,1},{5,3},{7,5},{10,8},{12,10},{14,12},{11,9},... | collective-permute-start | bytes 7352 | tf_op jit(solution)/shard_map/ppermute | solution.py:29
  58.3 3.1 %collective-permute-start.7 = (f32[16,128]{1,0:T(8,128)S(1)}, f32[16,128]{1,0:T(8,128)S(1)}, u32[]{:S(2)}, u32[]{:S(2)}) collective-permute-start(f32[16,128]{1,0:T(8,128)S(1)} %fusion.153), channel_id=1, source_target_pairs={{0,1},{1,0},{2,3},{3,2},{4,5},{5,4},{6,7},{7,6},{8,9},{9,8},{10,11... | collective-permute-start | bytes 24584 | tf_op jit(solution)/shard_map/ppermute | solution.py:16
  61.4 12.5 %collective-permute-start.8 = (f32[34,1,128]{2,1,0:T(1,128)S(1)}, f32[34,1,128]{2,1,0:T(1,128)S(1)}, u32[]{:S(2)}, u32[]{:S(2)}) collective-permute-start(f32[34,1,128]{2,1,0:T(1,128)S(1)} %get-tuple-element.49), channel_id=1, source_target_pairs={{0,8},{8,16},{16,24},{24,32},{32,40},{40,48},{48,56},{56,64},{64,7... | collective-permute-start | bytes 52232 | tf_op jit(solution)/shard_map/ppermute | solution.py:27
  63.3 11.4 %collective-permute-start.9 = (f32[34,1,128]{2,1,0:T(1,128)S(1)}, f32[34,1,128]{2,1,0:T(1,128)S(1)}, u32[]{:S(2)}, u32[]{:S(2)}) collective-permute-start(f32[34,1,128]{2,1,0:T(1,128)S(1)} %get-tuple-element.50), channel_id=1, source_target_pairs={{8,0},{16,8},{24,16},{32,24},{40,32},{48,40},{56,48},{64,56},{72,6... | collective-permute-start | bytes 52232 | tf_op jit(solution)/shard_map/ppermute | solution.py:29
  75.0 10.6 %collective-permute-start.10 = (f32[34,18,1]{2,1,0:T(8,128)S(1)}, f32[34,18,1]{2,1,0:T(8,128)S(1)}, u32[]{:S(2)}, u32[]{:S(2)}) collective-permute-start(f32[34,18,1]{2,1,0:T(8,128)S(1)} %get-tuple-element.31), channel_id=1, source_target_pairs={{0,2},{2,4},{4,6},{1,3},{3,5},{5,7},{8,10},{10,12},{12,14},{9,11},... | collective-permute-start | bytes 7352 | tf_op jit(solution)/shard_map/ppermute | solution.py:27
  77.9 11.6 %collective-permute-start.11 = (f32[34,18,1]{2,1,0:T(8,128)S(1)}, f32[34,18,1]{2,1,0:T(8,128)S(1)}, u32[]{:S(2)}, u32[]{:S(2)}) collective-permute-start(f32[34,18,1]{2,1,0:T(8,128)S(1)} %get-tuple-element.32), channel_id=1, source_target_pairs={{2,0},{4,2},{6,4},{3,1},{5,3},{7,5},{10,8},{12,10},{14,12},{11,9},... | collective-permute-start | bytes 7352 | tf_op jit(solution)/shard_map/ppermute | solution.py:29
  102.2 3.1 %collective-permute-start.12 = (f32[16,128]{1,0:T(8,128)S(1)}, f32[16,128]{1,0:T(8,128)S(1)}, u32[]{:S(2)}, u32[]{:S(2)}) collective-permute-start(f32[16,128]{1,0:T(8,128)S(1)} %fusion.154), channel_id=1, source_target_pairs={{0,1},{1,0},{2,3},{3,2},{4,5},{5,4},{6,7},{7,6},{8,9},{9,8},{10,11... | collective-permute-start | bytes 24584 | tf_op jit(solution)/shard_map/ppermute | solution.py:16
  105.4 12.5 %collective-permute-start.13 = (f32[34,1,128]{2,1,0:T(1,128)S(1)}, f32[34,1,128]{2,1,0:T(1,128)S(1)}, u32[]{:S(2)}, u32[]{:S(2)}) collective-permute-start(f32[34,1,128]{2,1,0:T(1,128)S(1)} %get-tuple-element.45), channel_id=1, source_target_pairs={{0,8},{8,16},{16,24},{24,32},{32,40},{40,48},{48,56},{56,64},{64,7... | collective-permute-start | bytes 52232 | tf_op jit(solution)/shard_map/ppermute | solution.py:27
  107.3 11.4 %collective-permute-start.14 = (f32[34,1,128]{2,1,0:T(1,128)S(1)}, f32[34,1,128]{2,1,0:T(1,128)S(1)}, u32[]{:S(2)}, u32[]{:S(2)}) collective-permute-start(f32[34,1,128]{2,1,0:T(1,128)S(1)} %get-tuple-element.46), channel_id=1, source_target_pairs={{8,0},{16,8},{24,16},{32,24},{40,32},{48,40},{56,48},{64,56},{72,6... | collective-permute-start | bytes 52232 | tf_op jit(solution)/shard_map/ppermute | solution.py:29
  119.0 10.5 %collective-permute-start.15 = (f32[34,18,1]{2,1,0:T(8,128)S(1)}, f32[34,18,1]{2,1,0:T(8,128)S(1)}, u32[]{:S(2)}, u32[]{:S(2)}) collective-permute-start(f32[34,18,1]{2,1,0:T(8,128)S(1)} %get-tuple-element.29), channel_id=1, source_target_pairs={{0,2},{2,4},{4,6},{1,3},{3,5},{5,7},{8,10},{10,12},{12,14},{9,11},... | collective-permute-start | bytes 7352 | tf_op jit(solution)/shard_map/ppermute | solution.py:27
  121.7 11.6 %collective-permute-start.16 = (f32[34,18,1]{2,1,0:T(8,128)S(1)}, f32[34,18,1]{2,1,0:T(8,128)S(1)}, u32[]{:S(2)}, u32[]{:S(2)}) collective-permute-start(f32[34,18,1]{2,1,0:T(8,128)S(1)} %get-tuple-element.30), channel_id=1, source_target_pairs={{2,0},{4,2},{6,4},{3,1},{5,3},{7,5},{10,8},{12,10},{14,12},{11,9},... | collective-permute-start | bytes 7352 | tf_op jit(solution)/shard_map/ppermute | solution.py:29
  146.0 3.1 %collective-permute-start.17 = (f32[16,128]{1,0:T(8,128)S(1)}, f32[16,128]{1,0:T(8,128)S(1)}, u32[]{:S(2)}, u32[]{:S(2)}) collective-permute-start(f32[16,128]{1,0:T(8,128)S(1)} %fusion.155), channel_id=1, source_target_pairs={{0,1},{1,0},{2,3},{3,2},{4,5},{5,4},{6,7},{7,6},{8,9},{9,8},{10,11... | collective-permute-start | bytes 24584 | tf_op jit(solution)/shard_map/ppermute | solution.py:16
  149.1 12.6 %collective-permute-start.18 = (f32[34,1,128]{2,1,0:T(1,128)S(1)}, f32[34,1,128]{2,1,0:T(1,128)S(1)}, u32[]{:S(2)}, u32[]{:S(2)}) collective-permute-start(f32[34,1,128]{2,1,0:T(1,128)S(1)} %get-tuple-element.41), channel_id=1, source_target_pairs={{0,8},{8,16},{16,24},{24,32},{32,40},{40,48},{48,56},{56,64},{64,7... | collective-permute-start | bytes 52232 | tf_op jit(solution)/shard_map/ppermute | solution.py:27
  151.1 11.4 %collective-permute-start.19 = (f32[34,1,128]{2,1,0:T(1,128)S(1)}, f32[34,1,128]{2,1,0:T(1,128)S(1)}, u32[]{:S(2)}, u32[]{:S(2)}) collective-permute-start(f32[34,1,128]{2,1,0:T(1,128)S(1)} %get-tuple-element.42), channel_id=1, source_target_pairs={{8,0},{16,8},{24,16},{32,24},{40,32},{48,40},{56,48},{64,56},{72,6... | collective-permute-start | bytes 52232 | tf_op jit(solution)/shard_map/ppermute | solution.py:29
  162.8 14.4 %collective-permute-start.20 = (f32[34,18,1]{2,1,0:T(8,128)S(1)}, f32[34,18,1]{2,1,0:T(8,128)S(1)}, u32[]{:S(2)}, u32[]{:S(2)}) collective-permute-start(f32[34,18,1]{2,1,0:T(8,128)S(1)} %get-tuple-element.27), channel_id=1, source_target_pairs={{0,2},{2,4},{4,6},{1,3},{3,5},{5,7},{8,10},{10,12},{12,14},{9,11},... | collective-permute-start | bytes 7352 | tf_op jit(solution)/shard_map/ppermute | solution.py:27
  164.8 11.8 %collective-permute-start.21 = (f32[34,18,1]{2,1,0:T(8,128)S(1)}, f32[34,18,1]{2,1,0:T(8,128)S(1)}, u32[]{:S(2)}, u32[]{:S(2)}) collective-permute-start(f32[34,18,1]{2,1,0:T(8,128)S(1)} %get-tuple-element.28), channel_id=1, source_target_pairs={{2,0},{4,2},{6,4},{3,1},{5,3},{7,5},{10,8},{12,10},{14,12},{11,9},... | collective-permute-start | bytes 7352 | tf_op jit(solution)/shard_map/ppermute | solution.py:29
  (3 other events, 51.1 us)
where the time goes:
time: 194 us; the launch traced here: 192 us
  starting transfers between devices  83.9 us (43%)
  waiting for transfers between devices  45 us (23%)
  blocking collectives  39.4 us (20%)
  other arithmetic  16.6 us (9%)
  matrix products  3.22 us (2%)
  local copies, waits for them, and re-layouts  2.89 us (1%)
    ppermute x8, starting transfers between devices, extended_2(): lax.ppermute(head, axis, [((i + 1) % count, i) for i in range(ends)])  50.9 us
    ppermute x8, waiting for transfers between devices, extended_2(): lax.ppermute(head, axis, [((i + 1) % count, i) for i in range(ends)])  24.4 us
    ppermute x8, starting transfers between devices, extended_2(): lax.ppermute(tail, axis, [(i, (i + 1) % count) for i in range(ends)])  19.2 us
    ppermute x8, waiting for transfers between devices, extended_2(): lax.ppermute(tail, axis, [(i, (i + 1) % count) for i in range(ends)])  18.1 us
    all_to_all x3, blocking collectives, per_device(): lax.all_to_all(defect, 'vert', split_axis=1, concat_axis=0, tiled=True)  17.8 us
    all_to_all x4, blocking collectives, to_slabs(): lax.all_to_all(increment, 'vert', split_axis=0, concat_axis=1, tiled=True)  15.8 us
    ppermute x6, starting transfers between devices, partner(): return lax.ppermute(block, axis, route)  13.8 us
    all_to_all x1, blocking collectives, per_device(): lax.all_to_all(residual, 'vert', split_axis=1, concat_axis=0, tiled=True)  5.92 us
  transfers between devices with their start and end apart: 22, of which 15 were waited for; matrix products, arithmetic and copies ran while one was open for 2% of the time, Pallas kernels for 0%

commit v1 on v0

v1 whole, which is shorter than its diff:
```python
import jax
import jax.numpy as jnp
from jax import lax
from jax.experimental import pallas as pl
from jax.experimental.pallas import tpu as pltpu
from jax.sharding import PartitionSpec as P

SWEEPS = 4
MESH = pl.DeviceIdType.MESH
F32 = jnp.float32
BF16 = jnp.bfloat16


def kernel(
    pot_hbm, src_hbm, sten_hbm, surf_hbm, elev_hbm, hull_hbm, cinv_hbm,
    upd_hbm, res_hbm,
    pot, srcl, sten, surf, elev, hullm, cinv,
    coef, edge, shifted, field, applied, resid, corr, hull, weight, top, lhs, ghost3, outl,
    rows_s, rows_r, packs_s, packs_r, diag_s, diag_r,
    lsem, xs_sem, xr_sem, row_ss, row_rs, pack_ss, pack_rs, diag_ss, diag_rs, out_ss, out_rs, out_ls,
):
    s = lax.axis_index("ship")
    t = lax.axis_index("trans")
    v = lax.axis_index("vert")
    ships = lax.axis_size("ship")
    transes = lax.axis_size("trans")
    slow_ok = jnp.where(v == 0, s > 0, s < ships - 1)
    role_ok = (slow_ok, s >= 0)
    role_dev = ((s + 2 * v - 1, 1 - v), (s, 1 - v))
    side_ok = (t > 0, t < transes - 1)
    side_t = (t - 1, t + 1)
    edge_x = (7 * v, 7 * (1 - v))
    edge_b = (2 * v, 2 * (1 - v))

    def clear(k, _):
        for role in range(2):
            rows_r[k, role] = jnp.zeros((80, 128), F32)
            packs_r[k, role] = jnp.zeros((8, 128), F32)
            diag_r[k, role] = jnp.zeros((16, 128), F32)
        return 0

    lax.fori_loop(0, SWEEPS, clear, 0)

    barrier = pltpu.get_barrier_semaphore()
    count = 0
    for role in range(2):
        ship, vert = role_dev[role]
        for ok, tt in ((role_ok[role], t), (role_ok[role] & side_ok[0], t - 1), (role_ok[role] & side_ok[1], t + 1)):

            @pl.when(ok)
            def _():
                pl.semaphore_signal(barrier, inc=1, device_id=(ship, tt, vert), device_id_type=MESH)

            count = count + ok.astype(jnp.int32)
    for side in range(2):

        @pl.when(side_ok[side])
        def _():
            pl.semaphore_signal(barrier, inc=1, device_id=(s, side_t[side], v), device_id_type=MESH)

        count = count + side_ok[side].astype(jnp.int32)

    own = pl.ds(pl.multiple_of(8 * v, 8), 8)
    other = pl.ds(pl.multiple_of(8 * (1 - v), 8), 8)
    levels = pl.ds(32 * v, 32)
    local = [
        pltpu.make_async_copy(pot_hbm.at[:, own], pot.at[levels], lsem.at[0]),
        pltpu.make_async_copy(hull_hbm, hullm, lsem.at[1]),
        pltpu.make_async_copy(surf_hbm, surf, lsem.at[2]),
        pltpu.make_async_copy(sten_hbm.at[:, :, own], sten.at[:, levels], lsem.at[3]),
        pltpu.make_async_copy(src_hbm.at[:, own], srcl.at[levels], lsem.at[4]),
        pltpu.make_async_copy(elev_hbm, elev, lsem.at[5]),
        pltpu.make_async_copy(cinv_hbm, cinv, lsem.at[6]),
    ]
    for copy in local:
        copy.start()

    pl.semaphore_wait(barrier, count)

    partner = (s, t, 1 - v)
    cross = [
        pltpu.make_async_remote_copy(
            src, dst, xs_sem.at[i], xr_sem.at[i], device_id=partner, device_id_type=MESH
        )
        for i, (src, dst) in enumerate(
            (
                (pot_hbm.at[:, other], pot.at[levels]),
                (sten_hbm.at[:, :, other], sten.at[:, levels]),
                (src_hbm.at[:, other], srcl.at[levels]),
            )
        )
    ]
    for copy in cross:
        copy.start()

    lane = lax.broadcasted_iota(jnp.int32, (8, 128), 1)
    sub = lax.broadcasted_iota(jnp.int32, (8, 128), 0)

    def row_copy(k, role):
        return pltpu.make_async_remote_copy(
            rows_s.at[k, role], rows_r.at[k, role], row_ss.at[k, role], row_rs.at[k, role],
            device_id=(role_dev[role][0], t, role_dev[role][1]), device_id_type=MESH,
        )

    def pack_copy(k, side):
        return pltpu.make_async_remote_copy(
            packs_s.at[k, side], packs_r.at[k, 1 - side], pack_ss.at[k, side], pack_rs.at[k, 1 - side],
            device_id=(s, side_t[side], v), device_id_type=MESH,
        )

    def diag_copy(k, role, side):
        return pltpu.make_async_remote_copy(
            diag_s.at[k, role], diag_r.at[k, role, pl.ds(8 * (1 - side), 8)],
            diag_ss.at[k, role, side], diag_rs.at[k, role, 1 - side],
            device_id=(role_dev[role][0], side_t[side], role_dev[role][1]), device_id_type=MESH,
        )

    def send_row(k, role, line, top_line):
        whole = jnp.concatenate(
            [
                jnp.broadcast_to(line[0:1], (8, 128)),
                line,
                jnp.broadcast_to(top_line, (8, 128)),
                jnp.zeros((48, 128), F32),
            ],
            axis=0,
        )
        rows_s[k, role] = whole[0:80]

        @pl.when(role_ok[role])
        def _():
            row_copy(k, role).start()

        turned = jnp.transpose(whole)
        diag_s[k, role] = jnp.concatenate(
            [turned[0:1], turned[127:128], jnp.zeros((6, 128), F32)], axis=0
        )
        for side in range(2):

            @pl.when(role_ok[role] & side_ok[side])
            def _():
                diag_copy(k, role, side).start()

    def send_packs(k):
        def one(z, carry):
            left, right = carry
            turned = pltpu.roll(field[pl.ds(pl.multiple_of(8 * z + 8, 8), 8), :], z, 1)
            left = jnp.where(lane == z, turned, left)
            right = jnp.where(lane == (z + 127) % 128, turned, right)
            return left, right

        zero = jnp.zeros((8, 128), F32)
        left, right = lax.fori_loop(0, 65, one, (zero, zero), unroll=5)
        packs_s[k, 0] = left
        packs_s[k, 1] = pltpu.roll(right, 1, 1)
        for side in range(2):

            @pl.when(side_ok[side])
            def _():
                pack_copy(k, side).start()

    def close_field():
        field[0:8, :] = field[8:16, :]
        field[520:528, :] = hull[...] * field[512:520, :] + top[...]

    def column(ref, x, first):
        return ref[pl.ds(x + first, 64, stride=8), :]

    local[0].wait()
    local[1].wait()
    local[2].wait()
    hull[...] = hullm[...].astype(F32)
    top[...] = (1.0 - hull[...]) * surf[...]
    cross[0].wait_recv()
    field[8:520, :] = pot[...].reshape(512, 128)
    close_field()
    for role in range(2):
        x = edge_x[role]
        send_row(0, role, column(field, x, 8), field[pl.ds(x + 520, 1), :])
    send_packs(0)

    local[5].wait()
    local[6].wait()
    weight[...] = 0.5 * (1.0 + elev[...]) * (1.0 + elev[...])
    both = cinv[...].reshape(128, 64)
    high = both.astype(BF16).astype(F32)
    lhs[...] = jnp.concatenate([high, high, both - high], axis=1).astype(BF16)
    local[4].wait()
    cross[2].wait_recv()
    applied[...] = srcl[...].reshape(512, 128)
    for x in range(8):
        resid[x] = column(applied, x, 0)
        corr[x] = jnp.zeros((64, 128), F32)
    local[3].wait()
    cross[1].wait_recv()

    def widen(o, _):
        def block(i, _):
            coef[o, pl.ds(pl.multiple_of(64 * i, 64), 64), :] = (
                sten[o, pl.ds(8 * i, 8)].astype(F32).reshape(64, 128)
            )
            return 0

        return lax.fori_loop(0, 8, block, 0, unroll=True)

    lax.fori_loop(0, 27, widen, 0)
    for role in range(2):
        for a in range(3):
            for c in range(3):
                o = 9 * a + 3 * edge_b[role] + c
                edge[role, 3 * a + c] = coef[o, pl.ds(edge_x[role], 64, stride=8), :]

    def solve(u, hull_line):
        hi = u.astype(BF16)
        lo = (u - hi.astype(F32)).astype(BF16)
        y = jnp.dot(lhs[...], jnp.concatenate([hi, lo, hi], axis=0), preferred_element_type=F32)
        return jnp.where(hull_line > 0.5, y[64:128], y[0:64])

    lane80 = lax.broadcasted_iota(jnp.int32, (80, 128), 1)

    def ghost_part(k, role):
        @pl.when(role_ok[role])
        def _():
            row_copy(k, role).wait_recv()

        for side in range(2):

            @pl.when(role_ok[role] & side_ok[side])
            def _():
                diag_copy(k, role, 1 - side).wait_recv()

        line = rows_r[k, role]
        turned = jnp.transpose(
            jnp.concatenate([diag_r[k, role], jnp.zeros((112, 128), F32)], axis=0)
        )
        ghost3[0] = jnp.where(lane80 == 0, turned[0:80, 1:2], pltpu.roll(line, 1, 1))
        ghost3[1] = line
        ghost3[2] = jnp.where(lane80 == 127, turned[0:80, 8:9], pltpu.roll(line, 127, 1))
        total = jnp.zeros((64, 128), F32)
        for a in range(3):
            for c in range(3):
                total = total + edge[role, 3 * a + c] * ghost3[c, 7 + a : 71 + a, :]
        return total

    def out_copies(i, hbm):
        mine = pltpu.make_async_copy(outl.at[i, levels], hbm.at[:, own], out_ls.at[i])
        theirs = pltpu.make_async_remote_copy(
            outl.at[i, pl.ds(32 * (1 - v), 32)], hbm.at[:, own], out_ss.at[i], out_rs.at[i],
            device_id=partner, device_id_type=MESH,
        )
        return mine, theirs

    def sweep(k, _):
        for side in range(2):

            @pl.when(side_ok[side])
            def _():
                pack_copy(k, 1 - side).wait_recv()

        from_left = packs_r[k, 0]
        from_right = packs_r[k, 1]

        def shift(z, _):
            here = pl.ds(pl.multiple_of(8 * z, 8), 8)
            level = jnp.clip(z - 1, 0, 64)
            middle = field[here, :]
            left = jnp.where(lane == 0, pltpu.roll(from_left, (128 - level) % 128, 1), pltpu.roll(middle, 1, 1))
            right = jnp.where(lane == 127, pltpu.roll(from_right, 127 - level, 1), pltpu.roll(middle, 127, 1))
            for c, value in enumerate((left, middle, right)):
                shifted[c, here, :] = jnp.where(sub == 0, 0.0, pltpu.roll(value, 1, 0))
                shifted[3 + c, here, :] = value
                shifted[6 + c, here, :] = jnp.where(sub == 7, 0.0, pltpu.roll(value, 7, 0))
            return 0

        lax.fori_loop(0, 66, shift, 0, unroll=3)

        def block(i, _):
            at = pl.multiple_of(64 * i, 64)
            total = jnp.zeros((64, 128), F32)
            for b in range(3):
                for c in range(3):
                    window = shifted[3 * b + c, pl.ds(at, 80), :]
                    for a in range(3):
                        total = total + coef[9 * a + 3 * b + c, pl.ds(at, 64), :] * window[8 * a : 8 * a + 64]
            applied[pl.ds(at, 64), :] = total
            return 0

        lax.fori_loop(0, 8, block, 0)

        part = ghost_part(k, 1)
        resid_x = edge_x[1]
        applied[pl.ds(resid_x, 64, stride=8), :] = column(applied, resid_x, 0) + part

        for pair in range(4):
            lines = []
            for x in (2 * pair, 2 * pair + 1):
                u = resid[x] - column(applied, x, 0)

                @pl.when(k == 0)
                def _():
                    resid[x] = u

                lines.append(u)
            u = jnp.concatenate(lines, axis=1)
            mask = jnp.concatenate([hull[2 * pair : 2 * pair + 1], hull[2 * pair + 1 : 2 * pair + 2]], axis=1)
            step = solve(u, mask)
            for i, x in enumerate((2 * pair, 2 * pair + 1)):
                corr[x] = corr[x] + weight[x : x + 1] * step[:, 128 * i : 128 * i + 128]

        part = ghost_part(k, 0)
        x = edge_x[0]

        @pl.when(k == 0)
        def _():
            resid[x] = resid[x] - part
            top[...] = jnp.zeros((8, 128), F32)

        line_hull = hull[pl.ds(x, 1), :]
        corr[x] = corr[x] - weight[pl.ds(x, 1), :] * solve(part, line_hull)

        @pl.when(k < SWEEPS - 1)
        def _():
            for role in range(2):
                x = edge_x[role]
                line = corr[x]
                send_row(k + 1, role, line, hull[pl.ds(x, 1), :] * line[63:64])

        for x in range(8):
            field[pl.ds(8 + x, 64, stride=8), :] = corr[x]
        close_field()

        @pl.when(k < SWEEPS - 1)
        def _():
            send_packs(k + 1)

        @pl.when(k == 0)
        def _():
            for x in range(8):
                applied[pl.ds(x, 64, stride=8), :] = resid[x]
            outl[0] = applied[...].reshape(64, 8, 128)
            for copy in out_copies(0, res_hbm):
                copy.start()

        return 0

    lax.fori_loop(0, SWEEPS, sweep, 0)

    outl[1] = pot[...] + field[8:520, :].reshape(64, 8, 128)
    for copy in out_copies(1, upd_hbm):
        copy.start()

    for copy in cross:
        copy.wait_send()

    def drain(k, _):
        for role in range(2):

            @pl.when(role_ok[role])
            def _():
                row_copy(k, role).wait_send()

            @pl.when(side_ok[role])
            def _():
                pack_copy(k, role).wait_send()

            for side in range(2):

                @pl.when(role_ok[role] & side_ok[side])
                def _():
                    diag_copy(k, role, side).wait_send()

        return 0

    lax.fori_loop(0, SWEEPS, drain, 0)
    for i, hbm in enumerate((res_hbm, upd_hbm)):
        mine, theirs = out_copies(i, hbm)
        mine.wait()
        theirs.wait_send()
        pltpu.make_async_remote_copy(
            outl.at[i, levels], hbm.at[:, other], out_ss.at[i], out_rs.at[i],
            device_id=partner, device_id_type=MESH,
        ).wait_recv()


def per_device(potential, source, stencil, surface_potential, elevation, hull_mask, column_inverse):
    vm = pltpu.VMEM
    dma = pltpu.SemaphoreType.DMA
    n = SWEEPS
    return pl.pallas_call(
        kernel,
        out_shape=(jax.ShapeDtypeStruct((32, 16, 128), F32), jax.ShapeDtypeStruct((32, 16, 128), F32)),
        in_specs=[pl.BlockSpec(memory_space=pl.ANY)] * 7,
        out_specs=(pl.BlockSpec(memory_space=pl.ANY), pl.BlockSpec(memory_space=pl.ANY)),
        scratch_shapes=[
            vm((64, 8, 128), F32), vm((64, 8, 128), F32), vm((27, 64, 8, 128), BF16), vm((8, 128), F32), vm((8, 128), F32),
            vm((8, 128), jnp.int32), vm((2, 64, 64), F32),
            vm((27, 512, 128), F32), vm((2, 9, 64, 128), F32), vm((9, 528, 128), F32), vm((528, 128), F32), vm((512, 128), F32),
            vm((8, 64, 128), F32), vm((8, 64, 128), F32), vm((8, 128), F32), vm((8, 128), F32), vm((8, 128), F32), vm((128, 192), BF16),
            vm((3, 80, 128), F32), vm((2, 64, 8, 128), F32),
            vm((n, 2, 80, 128), F32), vm((n, 2, 80, 128), F32), vm((n, 2, 8, 128), F32), vm((n, 2, 8, 128), F32),
            vm((n, 2, 8, 128), F32), vm((n, 2, 16, 128), F32),
            dma((7,)), dma((3,)), dma((3,)), dma((n, 2)), dma((n, 2)), dma((n, 2)), dma((n, 2)), dma((n, 2, 2)), dma((n, 2, 2)),
            dma((2,)), dma((2,)), dma((2,)),
        ],
        compiler_params=pltpu.CompilerParams(collective_id=0, has_side_effects=True, vmem_limit_bytes=60 * 1024 * 1024),
        name="defect_correction",
    )(potential, source, stencil, surface_potential, elevation, hull_mask, column_inverse)


def solution(mesh):
    return jax.shard_map(
        per_device,
        mesh=mesh,
        in_specs=(
            P("vert", "ship", "trans"),
            P("vert", "ship", "trans"),
            P(None, "vert", "ship", "trans"),
            P(("ship", "vert"), "trans"),
            P(("ship", "vert"), "trans"),
            P(("ship", "vert"), "trans"),
            P(),
        ),
        out_specs=(P("vert", "ship", "trans"), P("vert", "ship", "trans")),
        check_vma=False,
    )
```

time: 194 us -> 53 us (0.27)
  starting transfers between devices: 83.9 us -> 0 us
  Pallas kernels: 0 us -> 48.8 us
  waiting for transfers between devices: 45 us -> 0 us
  blocking collectives: 39.4 us -> 0 us
  other arithmetic: 16.6 us -> 0 us
  matrix products: 3.22 us -> 0 us
    ppermute x22 -> x0, starting transfers between devices: 83.9 us -> none  [the longest x8 50.9 us: extended_2(): lax.ppermute(head, axis, [((i + 1) % count, i) for i in range(ends)])]
    pallas_call x0 -> x1, Pallas kernels: none -> 48.8 us  [per_device(): pl.pallas_call(kernel, out_shape=(jax.ShapeDtypeStruct((32, 16, 128), F32...]
    ppermute x22 -> x0, waiting for transfers between devices: 45 us -> none  [the longest x8 24.4 us: extended_2(): lax.ppermute(head, axis, [((i + 1) % count, i) for i in range(ends)])]
    all_to_all x8 -> x0, blocking collectives: 39.4 us -> none  [the longest x3 17.8 us: per_device(): lax.all_to_all(defect, 'vert', split_axis=1, concat_axis=0, tiled=True)]
    concatenate x13 -> x0, other arithmetic: 4.3 us -> none  [the longest x12 4.28 us: extended_2(): jnp.concatenate([lax.ppermute(tail, axis, [(i, (i + 1) % count) for i in...]
    sub x4 -> x0, other arithmetic: 3.7 us -> none  [the longest x3 3.55 us: per_device(): defect = residual - stencil_apply(correction_pad, stencil)]
    dot_general x8 -> x0, matrix products: 3.22 us -> none  [the longest x4 1.61 us: project(): jnp.dot(column_inverse[0], flattened, precision=lax.Precision.HIGHEST, pr...]
    add x5 -> x0, other arithmetic: 3.09 us -> none  [the longest x2 2.27 us: stencil_apply(): summed = summed + stencil[offset_index].astype(jnp.float32) * window]
  transfers between devices with their start and end apart: 22 -> 0, of which waited for: 15 -> 0; matrix products, arithmetic and copies ran while one was open for 2% -> 0% of each run, Pallas kernels for 0% -> 0%
where the time goes in v1:
time: 53 us; the launch traced here: 52.8 us
  Pallas kernels  48.8 us (92%)
  local copies, waits for them, and re-layouts  3.34 us (6%)
  between operations  0.64 us (1%)
    pallas_call x1, Pallas kernels, per_device(): pl.pallas_call(kernel, out_shape=(jax.ShapeDtypeStruct((32, 16, 128), F32...  48.8 us
    unnamed x2, local copies, waits for them, and re-layouts  3.34 us

profile of v1, /device:TPU:7, one launch (start us, length us, event | category | flops | bytes accessed | tf_op | source)
XLA Modules:
  0.0 52.8 jit_solution(3042323207526179584)
XLA Ops:
  0.6 48.8 %defect_correction.1 = (f32[32,16,128]{2,1,0:T(8,128)}, f32[32,16,128]{2,1,0:T(8,128)}) custom-call(f32[32,16,128]{2,1,0:T(8,128)} %pot_hbm.1, f32[32,16,128]{2,1,0:T(8,128)} %src_hbm.1, bf16[27,32,16,128]{3,2,1,0:T(8,128)(2,1)} %sten_hbm.1, f32[8,128]{1,0:T(8,128)} %surf_hbm.1, f32[8,128]{1,0:T(8,128)} %elev_hbm.1, s32[8,128]{1,0:T(8,128)} %hull_hbm.1, ...), custom_call_target="tpu_custom_call" | custom-call | tf_op jit(solution)/shard_map/defect_correction/pallas_call | solution.py:389
  49.5 1.7 %copy.11 = f32[32,16,128]{2,1,0:T(8,128)} copy(f32[32,16,128]{2,1,0:T(8,128)} %get-tuple-element.4) | data formatting | bytes 524288
  51.1 1.7 %copy.12 = f32[32,16,128]{2,1,0:T(8,128)} copy(f32[32,16,128]{2,1,0:T(8,128)} %get-tuple-element.5) | data formatting | bytes 524288

commit v2 on v1

--- a/solution.py
+++ b/solution.py
@@ -17,6 +17,8 @@
     pot, srcl, sten, surf, elev, hullm, cinv,
     coef, edge, shifted, field, applied, resid, corr, hull, weight, top, lhs, ghost3, outl,
     rows_s, rows_r, packs_s, packs_r, diag_s, diag_r,
+    slab, line_s, prof_s, prof_r, rim_s, rim_r,
+    line_ss, line_rs, prof_ss, prof_rs, rim_ss, rim_rs,
     lsem, xs_sem, xr_sem, row_ss, row_rs, pack_ss, pack_rs, diag_ss, diag_rs, out_ss, out_rs, out_ls,
 ):
     s = lax.axis_index("ship")
@@ -40,12 +42,16 @@
         return 0
 
     lax.fori_loop(0, SWEEPS, clear, 0)
+    prof_r[...] = jnp.zeros_like(prof_r)
+    rim_r[...] = jnp.zeros_like(rim_r)
 
     barrier = pltpu.get_barrier_semaphore()
     count = 0
-    for role in range(2):
-        ship, vert = role_dev[role]
-        for ok, tt in ((role_ok[role], t), (role_ok[role] & side_ok[0], t - 1), (role_ok[role] & side_ok[1], t + 1)):
+    chip_ok = (s > 0, s < ships - 1)
+    chip_s = (s - 1, s + 1)
+    met = [(role_ok[role], *role_dev[role]) for role in range(2)] + [(chip_ok[i], chip_s[i], v) for i in range(2)]
+    for there, ship, vert in met:
+        for ok, tt in ((there, t), (there & side_ok[0], t - 1), (there & side_ok[1], t + 1)):
 
             @pl.when(ok)
             def _():
@@ -63,6 +69,8 @@
     own = pl.ds(pl.multiple_of(8 * v, 8), 8)
     other = pl.ds(pl.multiple_of(8 * (1 - v), 8), 8)
     levels = pl.ds(32 * v, 32)
+    whole_slab = pltpu.make_async_copy(pot_hbm, slab, lsem.at[7])
+    whole_slab.start()
     local = [
         pltpu.make_async_copy(pot_hbm.at[:, own], pot.at[levels], lsem.at[0]),
         pltpu.make_async_copy(hull_hbm, hullm, lsem.at[1]),
@@ -75,7 +83,65 @@
     for copy in local:
         copy.start()
 
+    lane = lax.broadcasted_iota(jnp.int32, (8, 128), 1)
+    sub = lax.broadcasted_iota(jnp.int32, (8, 128), 0)
+
+    def line_copy(dirn, core):
+        return pltpu.make_async_remote_copy(
+            line_s.at[dirn], rows_r.at[0, 0, pl.ds(pl.multiple_of(8 + 32 * core, 8), 32)],
+            line_ss.at[dirn], line_rs.at[core],
+            device_id=(chip_s[dirn], t, 1 - dirn), device_id_type=MESH,
+        )
+
+    def prof_copy(dirn, side, core):
+        return pltpu.make_async_remote_copy(
+            prof_s.at[dirn], prof_r.at[core, pl.ds(8 * (1 - side), 8)],
+            prof_ss.at[dirn, side], prof_rs.at[core, 1 - side],
+            device_id=(chip_s[dirn], side_t[side], 1 - dirn), device_id_type=MESH,
+        )
+
+    def rim_copy(place):
+        return pltpu.make_async_remote_copy(
+            rim_s, rim_r.at[(1, 0, 2)[place]], rim_ss.at[place], rim_rs.at[(1, 0, 2)[place]],
+            device_id=(role_dev[0][0], (side_t + (t,))[place], role_dev[0][1]), device_id_type=MESH,
+        )
+
+    rim_ok = (slow_ok & side_ok[0], slow_ok & side_ok[1], slow_ok)
+    whole_slab.wait()
+    first, last = slab[:, 0, :], slab[:, 15, :]
+    line_s[0] = first
+    line_s[1] = last
+    turned = jnp.transpose(jnp.concatenate([first, last, jnp.zeros((64, 128), F32)], axis=0))
+    ends = jnp.concatenate([turned[0:1], turned[127:128], jnp.zeros((6, 128), F32)], axis=0)
+    prof_s[0] = pltpu.roll(ends, 8 + 32 * v, 1)
+    prof_s[1] = pltpu.roll(ends, (104 + 32 * v) % 128, 1)
+    local[1].wait()
+    local[2].wait()
+    hull[...] = hullm[...].astype(F32)
+    top[...] = (1.0 - hull[...]) * surf[...]
+    rim_s[0:1] = hull[pl.ds(edge_x[0], 1), :]
+    rim_s[1:2] = top[pl.ds(edge_x[0], 1), :]
+    rim_s[2:8] = jnp.zeros((6, 128), F32)
+
     pl.semaphore_wait(barrier, count)
+
+    for dirn in range(2):
+
+        @pl.when(chip_ok[dirn])
+        def _():
+            line_copy(dirn, v).start()
+
+        for side in range(2):
+
+            @pl.when(chip_ok[dirn] & side_ok[side])
+            def _():
+                prof_copy(dirn, side, v).start()
+
+    for place in range(3):
+
+        @pl.when(rim_ok[place])
+        def _():
+            rim_copy(place).start()
 
     partner = (s, t, 1 - v)
     cross = [
@@ -92,9 +158,6 @@
     ]
     for copy in cross:
         copy.start()
-
-    lane = lax.broadcasted_iota(jnp.int32, (8, 128), 1)
-    sub = lax.broadcasted_iota(jnp.int32, (8, 128), 0)
 
     def row_copy(k, role):
         return pltpu.make_async_remote_copy(
@@ -142,15 +205,12 @@
                 diag_copy(k, role, side).start()
 
     def send_packs(k):
-        def one(z, carry):
-            left, right = carry
-            turned = pltpu.roll(field[pl.ds(pl.multiple_of(8 * z + 8, 8), 8), :], z, 1)
+        left = jnp.zeros((8, 128), F32)
+        right = left
+        for z in range(65):
+            turned = pltpu.roll(field[8 * z + 8 : 8 * z + 16, :], z, 1)
             left = jnp.where(lane == z, turned, left)
             right = jnp.where(lane == (z + 127) % 128, turned, right)
-            return left, right
-
-        zero = jnp.zeros((8, 128), F32)
-        left, right = lax.fori_loop(0, 65, one, (zero, zero), unroll=5)
         packs_s[k, 0] = left
         packs_s[k, 1] = pltpu.roll(right, 1, 1)
         for side in range(2):
@@ -166,18 +226,16 @@
     def column(ref, x, first):
         return ref[pl.ds(x + first, 64, stride=8), :]
 
-    local[0].wait()
-    local[1].wait()
-    local[2].wait()
-    hull[...] = hullm[...].astype(F32)
-    top[...] = (1.0 - hull[...]) * surf[...]
-    cross[0].wait_recv()
-    field[8:520, :] = pot[...].reshape(512, 128)
-    close_field()
-    for role in range(2):
-        x = edge_x[role]
-        send_row(0, role, column(field, x, 8), field[pl.ds(x + 520, 1), :])
-    send_packs(0)
+    def widen(core):
+        def one(o, _):
+            for i in range(4):
+                at = 32 * core + 8 * i
+                coef[o, pl.ds(pl.multiple_of(8 * at, 64), 64), :] = (
+                    sten[o, pl.ds(at, 8)].astype(F32).reshape(64, 128)
+                )
+            return 0
+
+        lax.fori_loop(0, 27, one, 0)
 
     local[5].wait()
     local[6].wait()
@@ -185,25 +243,24 @@
     both = cinv[...].reshape(128, 64)
     high = both.astype(BF16).astype(F32)
     lhs[...] = jnp.concatenate([high, high, both - high], axis=1).astype(BF16)
+    local[3].wait()
+    widen(v)
+
+    local[0].wait()
+    cross[0].wait_recv()
+    field[8:520, :] = pot[...].reshape(512, 128)
+    close_field()
+    send_row(0, 1, column(field, edge_x[1], 8), field[pl.ds(edge_x[1] + 520, 1), :])
+    send_packs(0)
+
     local[4].wait()
     cross[2].wait_recv()
     applied[...] = srcl[...].reshape(512, 128)
     for x in range(8):
         resid[x] = column(applied, x, 0)
         corr[x] = jnp.zeros((64, 128), F32)
-    local[3].wait()
     cross[1].wait_recv()
-
-    def widen(o, _):
-        def block(i, _):
-            coef[o, pl.ds(pl.multiple_of(64 * i, 64), 64), :] = (
-                sten[o, pl.ds(8 * i, 8)].astype(F32).reshape(64, 128)
-            )
-            return 0
-
-        return lax.fori_loop(0, 8, block, 0, unroll=True)
-
-    lax.fori_loop(0, 27, widen, 0)
+    widen(1 - v)
     for role in range(2):
         for a in range(3):
             for c in range(3):
@@ -218,16 +275,56 @@
 
     lane80 = lax.broadcasted_iota(jnp.int32, (80, 128), 1)
 
+    def gather_first():
+        for core in range(2):
+
+            @pl.when(slow_ok)
+            def _():
+                line_copy(0, core).wait_recv()
+
+            for side in range(2):
+
+                @pl.when(slow_ok & side_ok[side])
+                def _():
+                    prof_copy(0, 1 - side, core).wait_recv()
+
+        for place in range(3):
+
+            @pl.when(rim_ok[place])
+            def _():
+                rim_copy((1, 0, 2)[place]).wait_recv()
+
+        rows_r[0, 0, 0:8] = jnp.broadcast_to(rows_r[0, 0, 8:9], (8, 128))
+        rows_r[0, 0, 72:80] = jnp.broadcast_to(
+            rim_r[2, 0:1] * rows_r[0, 0, 71:72] + rim_r[2, 1:2], (8, 128)
+        )
+        for side in range(2):
+            part = pl.ds(8 * side, 8)
+            level = jnp.where(lane < 40, prof_r[0, part], prof_r[1, part])
+            level = jnp.where(lane == 7, pltpu.roll(level, 127, 1), level)
+            turn = (73, 72)[side]
+            rim_hull = pltpu.roll(jnp.broadcast_to(rim_r[side, 0:1], (8, 128)), turn, 1)
+            rim_top = pltpu.roll(jnp.broadcast_to(rim_r[side, 1:2], (8, 128)), turn, 1)
+            diag_r[0, 0, part] = jnp.where(lane == 72, rim_hull * pltpu.roll(level, 1, 1) + rim_top, level)
+
     def ghost_part(k, role):
-        @pl.when(role_ok[role])
+        here = role_ok[role] & (k > 0) if role == 0 else role_ok[role]
+
+        @pl.when(here)
         def _():
             row_copy(k, role).wait_recv()
 
         for side in range(2):
 
-            @pl.when(role_ok[role] & side_ok[side])
+            @pl.when(here & side_ok[side])
             def _():
                 diag_copy(k, role, 1 - side).wait_recv()
+
+        if role == 0:
+
+            @pl.when(k == 0)
+            def _():
+                gather_first()
 
         line = rows_r[k, role]
         turned = jnp.transpose(
@@ -272,7 +369,7 @@
                 shifted[6 + c, here, :] = jnp.where(sub == 7, 0.0, pltpu.roll(value, 7, 0))
             return 0
 
-        lax.fori_loop(0, 66, shift, 0, unroll=3)
+        lax.fori_loop(0, 66, shift, 0, unroll=11)
 
         def block(i, _):
             at = pl.multiple_of(64 * i, 64)
@@ -354,8 +451,9 @@
 
     def drain(k, _):
         for role in range(2):
-
-            @pl.when(role_ok[role])
+            sent = role_ok[role] & (k > 0) if role == 0 else role_ok[role]
+
+            @pl.when(sent)
             def _():
                 row_copy(k, role).wait_send()
 
@@ -365,13 +463,31 @@
 
             for side in range(2):
 
-                @pl.when(role_ok[role] & side_ok[side])
+                @pl.when(sent & side_ok[side])
                 def _():
                     diag_copy(k, role, side).wait_send()
 
         return 0
 
     lax.fori_loop(0, SWEEPS, drain, 0)
+    for dirn in range(2):
+
+        @pl.when(chip_ok[dirn])
+        def _():
+            line_copy(dirn, v).wait_send()
+
+        for side in range(2):
+
+            @pl.when(chip_ok[dirn] & side_ok[side])
+            def _():
+                prof_copy(dirn, side, v).wait_send()
+
+    for place in range(3):
+
+        @pl.when(rim_ok[place])
+        def _():
+            rim_copy(place).wait_send()
+
     for i, hbm in enumerate((res_hbm, upd_hbm)):
         mine, theirs = out_copies(i, hbm)
         mine.wait()
@@ -382,13 +498,24 @@
         ).wait_recv()
 
 
+def store(upd_vmem, res_vmem, upd_hbm, res_hbm, sem):
+    copies = [
+        pltpu.make_async_copy(upd_vmem, upd_hbm, sem.at[0]),
+        pltpu.make_async_copy(res_vmem, res_hbm, sem.at[1]),
+    ]
+    for copy in copies:
+        copy.start()
+    for copy in copies:
+        copy.wait()
+
+
 def per_device(potential, source, stencil, surface_potential, elevation, hull_mask, column_inverse):
     vm = pltpu.VMEM
     dma = pltpu.SemaphoreType.DMA
     n = SWEEPS
-    return pl.pallas_call(
+    held = pl.pallas_call(
         kernel,
-        out_shape=(jax.ShapeDtypeStruct((32, 16, 128), F32), jax.ShapeDtypeStruct((32, 16, 128), F32)),
+        out_shape=(vm((32, 16, 128), F32), vm((32, 16, 128), F32)),
         in_specs=[pl.BlockSpec(memory_space=pl.ANY)] * 7,
         out_specs=(pl.BlockSpec(memory_space=pl.ANY), pl.BlockSpec(memory_space=pl.ANY)),
         scratch_shapes=[
@@ -399,12 +526,22 @@
             vm((3, 80, 128), F32), vm((2, 64, 8, 128), F32),
             vm((n, 2, 80, 128), F32), vm((n, 2, 80, 128), F32), vm((n, 2, 8, 128), F32), vm((n, 2, 8, 128), F32),
             vm((n, 2, 8, 128), F32), vm((n, 2, 16, 128), F32),
-            dma((7,)), dma((3,)), dma((3,)), dma((n, 2)), dma((n, 2)), dma((n, 2)), dma((n, 2)), dma((n, 2, 2)), dma((n, 2, 2)),
+            vm((32, 16, 128), F32), vm((2, 32, 128), F32), vm((2, 8, 128), F32), vm((2, 16, 128), F32), vm((8, 128), F32), vm((3, 8, 128), F32),
+            dma((2,)), dma((2,)), dma((2, 2)), dma((2, 2)), dma((3,)), dma((3,)),
+            dma((8,)), dma((3,)), dma((3,)), dma((n, 2)), dma((n, 2)), dma((n, 2)), dma((n, 2)), dma((n, 2, 2)), dma((n, 2, 2)),
             dma((2,)), dma((2,)), dma((2,)),
         ],
         compiler_params=pltpu.CompilerParams(collective_id=0, has_side_effects=True, vmem_limit_bytes=60 * 1024 * 1024),
         name="defect_correction",
     )(potential, source, stencil, surface_potential, elevation, hull_mask, column_inverse)
+    return pl.pallas_call(
+        store,
+        out_shape=(jax.ShapeDtypeStruct((32, 16, 128), F32), jax.ShapeDtypeStruct((32, 16, 128), F32)),
+        in_specs=[pl.BlockSpec(memory_space=pltpu.VMEM)] * 2,
+        out_specs=(pl.BlockSpec(memory_space=pl.ANY), pl.BlockSpec(memory_space=pl.ANY)),
+        scratch_shapes=[dma((2,))],
+        name="store",
+    )(*[pltpu.with_memory_space_constraint(x, pltpu.VMEM) for x in held])
 
 
 def solution(mesh):

time: 53 us -> 47.8 us (0.902)
  the two profiles are of different devices: /device:TPU:7 before, /device:TPU:3 now
where the time goes in v2:
time: 47.8 us; the launch traced here: 47.7 us
  Pallas kernels  47 us (98%)
  between operations  0.64 us (1%)
    pallas_call x1, Pallas kernels, per_device(): pl.pallas_call(kernel, out_shape=(vm((32, 16, 128), F32), vm((32, 16, 128...  46.2 us

profile of v2, /device:TPU:3, one launch (start us, length us, event | category | flops | bytes accessed | tf_op | source)
XLA Modules:
  0.0 47.7 jit_solution(9905166047583973366)
XLA Ops:
  0.6 46.2 %defect_correction.1 = (f32[32,16,128]{2,1,0:T(8,128)S(1)}, f32[32,16,128]{2,1,0:T(8,128)S(1)}) custom-call(f32[32,16,128]{2,1,0:T(8,128)} %pot_hbm.1, f32[32,16,128]{2,1,0:T(8,128)} %src_hbm.1, bf16[27,32,16,128]{3,2,1,0:T(8,128)(2,1)} %sten_hbm.1, f32[8,128]{1,0:T(8,128)} %surf_hbm.1, f32[8,128]{1,0:T(8,128)} %elev_hbm.1, s32[8,128]{1,0:T(8,128)} %hull_hbm.1, ...), custom_call_target="tpu_custom_call" | custom-call | tf_op jit(solution)/shard_map/defect_correction/pallas_call | solution.py:516
  46.8 0.8 %store.1 = (f32[32,16,128]{2,1,0:T(8,128)}, f32[32,16,128]{2,1,0:T(8,128)}) custom-call(f32[32,16,128]{2,1,0:T(8,128)S(1)} %get-tuple-element.4.upd_vmem, f32[32,16,128]{2,1,0:T(8,128)S(1)} %get-tuple-element.5.res_vmem), custom_call_target="tpu_custom_call" | custom-call | tf_op jit(solution)/shard_map/store/pallas_call | solution.py:537

commit v3 on v2

--- a/solution.py
+++ b/solution.py
@@ -16,7 +16,7 @@
     upd_hbm, res_hbm,
     pot, srcl, sten, surf, elev, hullm, cinv,
     coef, edge, shifted, field, applied, resid, corr, hull, weight, top, lhs, ghost3, outl,
-    rows_s, rows_r, packs_s, packs_r, diag_s, diag_r,
+    far_s, far_r, far_sent, far_got, first_r, near_s, near_r, packs_s, packs_r, diag_s, diag_r,
     slab, line_s, prof_s, prof_r, rim_s, rim_r,
     line_ss, line_rs, prof_ss, prof_rs, rim_ss, rim_rs,
     lsem, xs_sem, xr_sem, row_ss, row_rs, pack_ss, pack_rs, diag_ss, diag_rs, out_ss, out_rs, out_ls,
@@ -34,17 +34,6 @@
     edge_x = (7 * v, 7 * (1 - v))
     edge_b = (2 * v, 2 * (1 - v))
 
-    def clear(k, _):
-        for role in range(2):
-            rows_r[k, role] = jnp.zeros((80, 128), F32)
-            packs_r[k, role] = jnp.zeros((8, 128), F32)
-            diag_r[k, role] = jnp.zeros((16, 128), F32)
-        return 0
-
-    lax.fori_loop(0, SWEEPS, clear, 0)
-    prof_r[...] = jnp.zeros_like(prof_r)
-    rim_r[...] = jnp.zeros_like(rim_r)
-
     barrier = pltpu.get_barrier_semaphore()
     count = 0
     chip_ok = (s > 0, s < ships - 1)
@@ -65,6 +54,28 @@
             pl.semaphore_signal(barrier, inc=1, device_id=(s, side_t[side], v), device_id_type=MESH)
 
         count = count + side_ok[side].astype(jnp.int32)
+
+    @pl.when(jnp.logical_not(slow_ok))
+    def _():
+        far_r[...] = jnp.zeros_like(far_r)
+        first_r[...] = jnp.zeros_like(first_r)
+        rim_r[2] = jnp.zeros((2, 1, 128), F32)
+
+    for side in range(2):
+
+        @pl.when(jnp.logical_not(side_ok[side]))
+        def _():
+            for k in range(SWEEPS):
+                packs_r[k, side] = jnp.zeros((8, 128), F32)
+                diag_r[k, 1, side] = jnp.zeros((1, 128), F32)
+
+        @pl.when(jnp.logical_not(slow_ok & side_ok[side]))
+        def _():
+            rim_r[side] = jnp.zeros((2, 1, 128), F32)
+            for core in range(2):
+                prof_r[core, side] = jnp.zeros((1, 128), F32)
+            for k in range(SWEEPS):
+                diag_r[k, 0, side] = jnp.zeros((1, 128), F32)
 
     own = pl.ds(pl.multiple_of(8 * v, 8), 8)
     other = pl.ds(pl.multiple_of(8 * (1 - v), 8), 8)
@@ -88,14 +99,14 @@
 
     def line_copy(dirn, core):
         return pltpu.make_async_remote_copy(
-            line_s.at[dirn], rows_r.at[0, 0, pl.ds(pl.multiple_of(8 + 32 * core, 8), 32)],
+            line_s.at[dirn], first_r.at[pl.ds(pl.multiple_of(32 * core, 32), 32)],
             line_ss.at[dirn], line_rs.at[core],
             device_id=(chip_s[dirn], t, 1 - dirn), device_id_type=MESH,
         )
 
     def prof_copy(dirn, side, core):
         return pltpu.make_async_remote_copy(
-            prof_s.at[dirn], prof_r.at[core, pl.ds(8 * (1 - side), 8)],
+            prof_s.at[dirn, side], prof_r.at[core, 1 - side],
             prof_ss.at[dirn, side], prof_rs.at[core, 1 - side],
             device_id=(chip_s[dirn], side_t[side], 1 - dirn), device_id_type=MESH,
         )
@@ -112,16 +123,16 @@
     line_s[0] = first
     line_s[1] = last
     turned = jnp.transpose(jnp.concatenate([first, last, jnp.zeros((64, 128), F32)], axis=0))
-    ends = jnp.concatenate([turned[0:1], turned[127:128], jnp.zeros((6, 128), F32)], axis=0)
-    prof_s[0] = pltpu.roll(ends, 8 + 32 * v, 1)
-    prof_s[1] = pltpu.roll(ends, (104 + 32 * v) % 128, 1)
+    for end, at in enumerate((0, 127)):
+        profile = turned[at : at + 1]
+        prof_s[0, end] = pltpu.roll(profile, 8 + 32 * v, 1)
+        prof_s[1, end] = pltpu.roll(profile, (104 + 32 * v) % 128, 1)
     local[1].wait()
     local[2].wait()
     hull[...] = hullm[...].astype(F32)
     top[...] = (1.0 - hull[...]) * surf[...]
-    rim_s[0:1] = hull[pl.ds(edge_x[0], 1), :]
-    rim_s[1:2] = top[pl.ds(edge_x[0], 1), :]
-    rim_s[2:8] = jnp.zeros((6, 128), F32)
+    rim_s[0] = hull[pl.ds(edge_x[0], 1), :]
+    rim_s[1] = top[pl.ds(edge_x[0], 1), :]
 
     pl.semaphore_wait(barrier, count)
 
@@ -160,8 +171,9 @@
         copy.start()
 
     def row_copy(k, role):
+        src, dst = ((far_s.at[k], far_r.at[k]), (near_s.at[k], near_r.at[k]))[role]
         return pltpu.make_async_remote_copy(
-            rows_s.at[k, role], rows_r.at[k, role], row_ss.at[k, role], row_rs.at[k, role],
+            src, dst, row_ss.at[k, role], row_rs.at[k, role],
             device_id=(role_dev[role][0], t, role_dev[role][1]), device_id_type=MESH,
         )
 
@@ -173,7 +185,7 @@
 
     def diag_copy(k, role, side):
         return pltpu.make_async_remote_copy(
-            diag_s.at[k, role], diag_r.at[k, role, pl.ds(8 * (1 - side), 8)],
+            diag_s.at[k, role, side], diag_r.at[k, role, 1 - side],
             diag_ss.at[k, role, side], diag_rs.at[k, role, 1 - side],
             device_id=(role_dev[role][0], side_t[side], role_dev[role][1]), device_id_type=MESH,
         )
@@ -188,16 +200,20 @@
             ],
             axis=0,
         )
-        rows_s[k, role] = whole[0:80]
+        if role == 0:
+            sent = (line - far_sent[...]).astype(BF16)
+            far_s[k] = sent
+            far_sent[...] = far_sent[...] + sent.astype(F32)
+        else:
+            near_s[k] = whole[8:80]
 
         @pl.when(role_ok[role])
         def _():
             row_copy(k, role).start()
 
         turned = jnp.transpose(whole)
-        diag_s[k, role] = jnp.concatenate(
-            [turned[0:1], turned[127:128], jnp.zeros((6, 128), F32)], axis=0
-        )
+        diag_s[k, role, 0] = turned[0:1]
+        diag_s[k, role, 1] = turned[127:128]
         for side in range(2):
 
             @pl.when(role_ok[role] & side_ok[side])
@@ -236,6 +252,9 @@
             return 0
 
         lax.fori_loop(0, 27, one, 0)
+
+    far_sent[...] = jnp.zeros((64, 128), F32)
+    far_got[...] = jnp.zeros((64, 128), F32)
 
     local[5].wait()
     local[6].wait()
@@ -294,18 +313,15 @@
             def _():
                 rim_copy((1, 0, 2)[place]).wait_recv()
 
-        rows_r[0, 0, 0:8] = jnp.broadcast_to(rows_r[0, 0, 8:9], (8, 128))
-        rows_r[0, 0, 72:80] = jnp.broadcast_to(
-            rim_r[2, 0:1] * rows_r[0, 0, 71:72] + rim_r[2, 1:2], (8, 128)
-        )
-        for side in range(2):
-            part = pl.ds(8 * side, 8)
-            level = jnp.where(lane < 40, prof_r[0, part], prof_r[1, part])
-            level = jnp.where(lane == 7, pltpu.roll(level, 127, 1), level)
+        for side in range(2):
+            level = jnp.where(lane[0:1] < 40, prof_r[0, side], prof_r[1, side])
+            level = jnp.where(lane[0:1] == 7, pltpu.roll(level, 127, 1), level)
             turn = (73, 72)[side]
-            rim_hull = pltpu.roll(jnp.broadcast_to(rim_r[side, 0:1], (8, 128)), turn, 1)
-            rim_top = pltpu.roll(jnp.broadcast_to(rim_r[side, 1:2], (8, 128)), turn, 1)
-            diag_r[0, 0, part] = jnp.where(lane == 72, rim_hull * pltpu.roll(level, 1, 1) + rim_top, level)
+            rim_hull = pltpu.roll(rim_r[side, 0], turn, 1)
+            rim_top = pltpu.roll(rim_r[side, 1], turn, 1)
+            diag_r[0, 0, side] = jnp.where(lane[0:1] == 72, rim_hull * pltpu.roll(level, 1, 1) + rim_top, level)
+        ghost3[1, 8:72, :] = first_r[...]
+        ghost3[1, 72:80, :] = jnp.broadcast_to(rim_r[2, 0] * first_r[63:64, :] + rim_r[2, 1], (8, 128))
 
     def ghost_part(k, role):
         here = role_ok[role] & (k > 0) if role == 0 else role_ok[role]
@@ -326,13 +342,22 @@
             def _():
                 gather_first()
 
-        line = rows_r[k, role]
+            @pl.when(k > 0)
+            def _():
+                line = far_got[...] + far_r[k].astype(F32)
+                far_got[...] = line
+                ghost3[1, 8:72, :] = line
+                ghost3[1, 72:80, :] = jnp.broadcast_to(rim_r[2, 0] * line[63:64], (8, 128))
+
+        else:
+            ghost3[1, 8:80, :] = near_r[k]
+        ghost3[1, 0:8, :] = jnp.broadcast_to(ghost3[1, 8:9, :], (8, 128))
+        line = ghost3[1]
         turned = jnp.transpose(
-            jnp.concatenate([diag_r[k, role], jnp.zeros((112, 128), F32)], axis=0)
-        )
-        ghost3[0] = jnp.where(lane80 == 0, turned[0:80, 1:2], pltpu.roll(line, 1, 1))
-        ghost3[1] = line
-        ghost3[2] = jnp.where(lane80 == 127, turned[0:80, 8:9], pltpu.roll(line, 127, 1))
+            jnp.concatenate([diag_r[k, role, 0], diag_r[k, role, 1], jnp.zeros((126, 128), F32)], axis=0)
+        )
+        ghost3[0] = jnp.where(lane80 == 0, turned[0:80, 0:1], pltpu.roll(line, 1, 1))
+        ghost3[2] = jnp.where(lane80 == 127, turned[0:80, 1:2], pltpu.roll(line, 127, 1))
         total = jnp.zeros((64, 128), F32)
         for a in range(3):
             for c in range(3):
@@ -404,6 +429,11 @@
             for i, x in enumerate((2 * pair, 2 * pair + 1)):
                 corr[x] = corr[x] + weight[x : x + 1] * step[:, 128 * i : 128 * i + 128]
 
+        @pl.when(k < SWEEPS - 1)
+        def _():
+            line = corr[edge_x[1]]
+            send_row(k + 1, 1, line, hull[pl.ds(edge_x[1], 1), :] * line[63:64])
+
         part = ghost_part(k, 0)
         x = edge_x[0]
 
@@ -413,14 +443,12 @@
             top[...] = jnp.zeros((8, 128), F32)
 
         line_hull = hull[pl.ds(x, 1), :]
-        corr[x] = corr[x] - weight[pl.ds(x, 1), :] * solve(part, line_hull)
+        line = corr[x] - weight[pl.ds(x, 1), :] * solve(part, line_hull)
+        corr[x] = line
 
         @pl.when(k < SWEEPS - 1)
         def _():
-            for role in range(2):
-                x = edge_x[role]
-                line = corr[x]
-                send_row(k + 1, role, line, hull[pl.ds(x, 1), :] * line[63:64])
+            send_row(k + 1, 0, line, line_hull * line[63:64])
 
         for x in range(8):
             field[pl.ds(8 + x, 64, stride=8), :] = corr[x]
@@ -524,9 +552,10 @@
             vm((27, 512, 128), F32), vm((2, 9, 64, 128), F32), vm((9, 528, 128), F32), vm((528, 128), F32), vm((512, 128), F32),
             vm((8, 64, 128), F32), vm((8, 64, 128), F32), vm((8, 128), F32), vm((8, 128), F32), vm((8, 128), F32), vm((128, 192), BF16),
             vm((3, 80, 128), F32), vm((2, 64, 8, 128), F32),
-            vm((n, 2, 80, 128), F32), vm((n, 2, 80, 128), F32), vm((n, 2, 8, 128), F32), vm((n, 2, 8, 128), F32),
-            vm((n, 2, 8, 128), F32), vm((n, 2, 16, 128), F32),
-            vm((32, 16, 128), F32), vm((2, 32, 128), F32), vm((2, 8, 128), F32), vm((2, 16, 128), F32), vm((8, 128), F32), vm((3, 8, 128), F32),
+            vm((n, 64, 128), BF16), vm((n, 64, 128), BF16), vm((64, 128), F32), vm((64, 128), F32), vm((64, 128), F32), vm((n, 72, 128), F32), vm((n, 72, 128), F32),
+            vm((n, 2, 8, 128), F32), vm((n, 2, 8, 128), F32), vm((n, 2, 2, 1, 128), F32), vm((n, 2, 2, 1, 128), F32),
+            vm((32, 16, 128), F32), vm((2, 32, 128), F32), vm((2, 2, 1, 128), F32), vm((2, 2, 1, 128), F32), vm((2, 1, 128), F32),
+            vm((3, 2, 1, 128), F32),
             dma((2,)), dma((2,)), dma((2, 2)), dma((2, 2)), dma((3,)), dma((3,)),
             dma((8,)), dma((3,)), dma((3,)), dma((n, 2)), dma((n, 2)), dma((n, 2)), dma((n, 2)), dma((n, 2, 2)), dma((n, 2, 2)),
             dma((2,)), dma((2,)), dma((2,)),

time: 47.8 us -> 45.1 us (0.944)
  the two profiles are of different devices: /device:TPU:3 before, /device:TPU:7 now
where the time goes in v3:
time: 45.1 us; the launch traced here: 44.9 us
  Pallas kernels  44.3 us (98%)
  between operations  0.64 us (1%)
    pallas_call x1, Pallas kernels, per_device(): pl.pallas_call(kernel, out_shape=(vm((32, 16, 128), F32), vm((32, 16, 128...  43.5 us

profile of v3, /device:TPU:7, one launch (start us, length us, event | category | flops | bytes accessed | tf_op | source)
XLA Modules:
  0.0 44.9 jit_solution(1420855543643148725)
XLA Ops:
  0.6 43.5 %defect_correction.1 = (f32[32,16,128]{2,1,0:T(8,128)S(1)}, f32[32,16,128]{2,1,0:T(8,128)S(1)}) custom-call(f32[32,16,128]{2,1,0:T(8,128)} %pot_hbm.1, f32[32,16,128]{2,1,0:T(8,128)} %src_hbm.1, bf16[27,32,16,128]{3,2,1,0:T(8,128)(2,1)} %sten_hbm.1, f32[8,128]{1,0:T(8,128)} %surf_hbm.1, f32[8,128]{1,0:T(8,128)} %elev_hbm.1, s32[8,128]{1,0:T(8,128)} %hull_hbm.1, ...), custom_call_target="tpu_custom_call" | custom-call | tf_op jit(solution)/shard_map/defect_correction/pallas_call | solution.py:544
  44.1 0.8 %store.1 = (f32[32,16,128]{2,1,0:T(8,128)}, f32[32,16,128]{2,1,0:T(8,128)}) custom-call(f32[32,16,128]{2,1,0:T(8,128)S(1)} %get-tuple-element.4.upd_vmem, f32[32,16,128]{2,1,0:T(8,128)S(1)} %get-tuple-element.5.res_vmem), custom_call_target="tpu_custom_call" | custom-call | tf_op jit(solution)/shard_map/store/pallas_call | solution.py:566

commit v4 on v3

--- a/solution.py
+++ b/solution.py
@@ -17,8 +17,8 @@
     pot, srcl, sten, surf, elev, hullm, cinv,
     coef, edge, shifted, field, applied, resid, corr, hull, weight, top, lhs, ghost3, outl,
     far_s, far_r, far_sent, far_got, first_r, near_s, near_r, packs_s, packs_r, diag_s, diag_r,
-    slab, line_s, prof_s, prof_r, rim_s, rim_r,
-    line_ss, line_rs, prof_ss, prof_rs, rim_ss, rim_rs,
+    tail, tail_r, slab, line_s, prof_s, prof_r, rim_s, rim_r,
+    tail_ss, tail_rs, line_ss, line_rs, prof_ss, prof_rs, rim_ss, rim_rs,
     lsem, xs_sem, xr_sem, row_ss, row_rs, pack_ss, pack_rs, diag_ss, diag_rs, out_ss, out_rs, out_ls,
 ):
     s = lax.axis_index("ship")
@@ -207,10 +207,6 @@
         else:
             near_s[k] = whole[8:80]
 
-        @pl.when(role_ok[role])
-        def _():
-            row_copy(k, role).start()
-
         turned = jnp.transpose(whole)
         diag_s[k, role, 0] = turned[0:1]
         diag_s[k, role, 1] = turned[127:128]
@@ -219,6 +215,10 @@
             @pl.when(role_ok[role] & side_ok[side])
             def _():
                 diag_copy(k, role, side).start()
+
+        @pl.when(role_ok[role])
+        def _():
+            row_copy(k, role).start()
 
     def send_packs(k):
         left = jnp.zeros((8, 128), F32)
@@ -372,6 +372,11 @@
         )
         return mine, theirs
 
+    tail_copy = pltpu.make_async_remote_copy(
+        tail.at[pl.ds(pl.multiple_of(32 * (1 - v), 32), 32)], tail_r, tail_ss, tail_rs,
+        device_id=partner, device_id_type=MESH,
+    )
+
     def sweep(k, _):
         for side in range(2):
 
@@ -434,6 +439,15 @@
             line = corr[edge_x[1]]
             send_row(k + 1, 1, line, hull[pl.ds(edge_x[1], 1), :] * line[63:64])
 
+        @pl.when(k == SWEEPS - 1)
+        def _():
+            for x in range(8):
+                field[pl.ds(8 + x, 64, stride=8), :] = corr[x]
+            applied[...] = pot[...].reshape(512, 128) + field[8:520, :]
+            outl[1] = applied[...].reshape(64, 8, 128)
+            for copy in out_copies(1, upd_hbm):
+                copy.start()
+
         part = ghost_part(k, 0)
         x = edge_x[0]
 
@@ -443,19 +457,24 @@
             top[...] = jnp.zeros((8, 128), F32)
 
         line_hull = hull[pl.ds(x, 1), :]
-        line = corr[x] - weight[pl.ds(x, 1), :] * solve(part, line_hull)
+        change = weight[pl.ds(x, 1), :] * solve(part, line_hull)
+        line = corr[x] - change
         corr[x] = line
 
+        @pl.when(k == SWEEPS - 1)
+        def _():
+            tail[...] = column(applied, x, 0) - change
+            tail_copy.start()
+
         @pl.when(k < SWEEPS - 1)
         def _():
             send_row(k + 1, 0, line, line_hull * line[63:64])
 
-        for x in range(8):
-            field[pl.ds(8 + x, 64, stride=8), :] = corr[x]
-        close_field()
-
         @pl.when(k < SWEEPS - 1)
         def _():
+            for x in range(8):
+                field[pl.ds(8 + x, 64, stride=8), :] = corr[x]
+            close_field()
             send_packs(k + 1)
 
         @pl.when(k == 0)
@@ -469,10 +488,6 @@
         return 0
 
     lax.fori_loop(0, SWEEPS, sweep, 0)
-
-    outl[1] = pot[...] + field[8:520, :].reshape(64, 8, 128)
-    for copy in out_copies(1, upd_hbm):
-        copy.start()
 
     for copy in cross:
         copy.wait_send()
@@ -524,6 +539,11 @@
             outl.at[i, levels], hbm.at[:, other], out_ss.at[i], out_rs.at[i],
             device_id=partner, device_id_type=MESH,
         ).wait_recv()
+    slab_rows = upd_hbm.reshape(512, 128)
+    slab_rows[pl.ds(15 * v, 32, stride=16), :] = tail[pl.ds(pl.multiple_of(32 * v, 32), 32), :]
+    tail_copy.wait_recv()
+    slab_rows[pl.ds(15 * (1 - v), 32, stride=16), :] = tail_r[...]
+    tail_copy.wait_send()
 
 
 def store(upd_vmem, res_vmem, upd_hbm, res_hbm, sem):
@@ -545,7 +565,7 @@
         kernel,
         out_shape=(vm((32, 16, 128), F32), vm((32, 16, 128), F32)),
         in_specs=[pl.BlockSpec(memory_space=pl.ANY)] * 7,
-        out_specs=(pl.BlockSpec(memory_space=pl.ANY), pl.BlockSpec(memory_space=pl.ANY)),
+        out_specs=(pl.BlockSpec(memory_space=pltpu.VMEM), pl.BlockSpec(memory_space=pltpu.VMEM)),
         scratch_shapes=[
             vm((64, 8, 128), F32), vm((64, 8, 128), F32), vm((27, 64, 8, 128), BF16), vm((8, 128), F32), vm((8, 128), F32),
             vm((8, 128), jnp.int32), vm((2, 64, 64), F32),
@@ -554,9 +574,9 @@
             vm((3, 80, 128), F32), vm((2, 64, 8, 128), F32),
             vm((n, 64, 128), BF16), vm((n, 64, 128), BF16), vm((64, 128), F32), vm((64, 128), F32), vm((64, 128), F32), vm((n, 72, 128), F32), vm((n, 72, 128), F32),
             vm((n, 2, 8, 128), F32), vm((n, 2, 8, 128), F32), vm((n, 2, 2, 1, 128), F32), vm((n, 2, 2, 1, 128), F32),
-            vm((32, 16, 128), F32), vm((2, 32, 128), F32), vm((2, 2, 1, 128), F32), vm((2, 2, 1, 128), F32), vm((2, 1, 128), F32),
+            vm((64, 128), F32), vm((32, 128), F32), vm((32, 16, 128), F32), vm((2, 32, 128), F32), vm((2, 2, 1, 128), F32), vm((2, 2, 1, 128), F32), vm((2, 1, 128), F32),
             vm((3, 2, 1, 128), F32),
-            dma((2,)), dma((2,)), dma((2, 2)), dma((2, 2)), dma((3,)), dma((3,)),
+            dma(()), dma(()), dma((2,)), dma((2,)), dma((2, 2)), dma((2, 2)), dma((3,)), dma((3,)),
             dma((8,)), dma((3,)), dma((3,)), dma((n, 2)), dma((n, 2)), dma((n, 2)), dma((n, 2)), dma((n, 2, 2)), dma((n, 2, 2)),
             dma((2,)), dma((2,)), dma((2,)),
         ],

time: 45.1 us -> 44.9 us (level)
  no operation moved by 1% of the time
where the time goes in v4:
time: 44.9 us; the launch traced here: 44.7 us
  Pallas kernels  44.1 us (98%)
  between operations  0.64 us (1%)
    pallas_call x1, Pallas kernels, per_device(): pl.pallas_call(kernel, out_shape=(vm((32, 16, 128), F32), vm((32, 16, 128...  43.3 us

profile of v4, /device:TPU:7, one launch (start us, length us, event | category | flops | bytes accessed | tf_op | source)
XLA Modules:
  0.0 44.7 jit_solution(14666011876744953367)
XLA Ops:
  0.6 43.3 %defect_correction.1 = (f32[32,16,128]{2,1,0:T(8,128)S(1)}, f32[32,16,128]{2,1,0:T(8,128)S(1)}) custom-call(f32[32,16,128]{2,1,0:T(8,128)} %pot_hbm.1, f32[32,16,128]{2,1,0:T(8,128)} %src_hbm.1, bf16[27,32,16,128]{3,2,1,0:T(8,128)(2,1)} %sten_hbm.1, f32[8,128]{1,0:T(8,128)} %surf_hbm.1, f32[8,128]{1,0:T(8,128)} %elev_hbm.1, s32[8,128]{1,0:T(8,128)} %hull_hbm.1, ...), custom_call_target="tpu_custom_call" | custom-call | tf_op jit(solution)/shard_map/defect_correction/pallas_call | solution.py:564
  43.9 0.8 %store.1 = (f32[32,16,128]{2,1,0:T(8,128)}, f32[32,16,128]{2,1,0:T(8,128)}) custom-call(f32[32,16,128]{2,1,0:T(8,128)S(1)} %get-tuple-element.4.upd_vmem, f32[32,16,128]{2,1,0:T(8,128)S(1)} %get-tuple-element.5.res_vmem), custom_call_target="tpu_custom_call" | custom-call | tf_op jit(solution)/shard_map/store/pallas_call | solution.py:586
